TPU v7x, 512 devices: a whole 4x4x16 slice. The times are simulated.
512 devices in a mesh: wide: 32 (over x, z_hi, core), narrow: 16 (over y, z_lo).
Axes of the slice: x: 4, y: 4, z: 16 (z_hi: 4, z_lo: 4; z = z_hi * 4 + z_lo), core: 2. Of those that a mesh axis runs over, the one named last changes fastest.
Arguments:
- features: bfloat16 [262144, 512], P(('wide', 'narrow')), may hold values from -6 to 6
- stripe_owner: int32 [16, 2], replicated, may hold values from 0 to 31
- dense_weight: int32 [262144, 1024], P(('wide', 'narrow')), may hold values from 0 to 3
- sparse_weight: int32 [512, 16, 128, 128], P(('wide', 'narrow')), may hold values from 0 to 3
- send_blocks: int32 [512, 16, 2], P(('wide', 'narrow')), may hold values from -1 to 3, as said below
- target_block: int32 [512, 16, 2], P(('wide', 'narrow')), may hold values from 0 to 3
- first_weight: bfloat16 [512, 2048], P('wide'), may hold values from -0.25 to 0.25
- second_weight: bfloat16 [2048, 512], P('wide'), may hold values from -0.125 to 0.125
Outputs:
- updated: bfloat16 [262144, 512], P(('wide', 'narrow'))
Inputs may be any that keep to these rules, and one draw needn't show every extreme that they name: `send_blocks`: entry [d, p, s] names a local row block of device d for slot s to partition p of d's wide group, -1 marks an empty slot, filled slots come first; in every wide group one partition receives 2 blocks from every member.
All inputs are finite; a program needn't handle non-finite values.
Results may differ from a plain program's by a relative error of at most 0.0057.
Values may be sent and summed in bfloat16 or wider, within the bound.
A program may use at most 128 MiB of HBM per device.

v0:
```python
import jax
import jax.numpy as jnp
from jax import lax
from jax.sharding import PartitionSpec as P


def padded_to(lines, count):
    spare = -len(lines) % count
    return jnp.pad(lines, [(0, spare)] + [(0, 0)] * (lines.ndim - 1))


def total_of(x, axis):
    lines = x.reshape(-1, *x.shape[1:][-1:])
    padded = padded_to(lines, lax.axis_size(axis))
    own = lax.psum_scatter(padded, axis, scatter_dimension=0, tiled=True)
    whole = lax.all_gather(own, axis, axis=0, tiled=True)
    return whole[: len(lines)].reshape(x.shape)


def tile_products(tile_weights, received):
    carried, present = received
    products = jnp.einsum(
        "pij,pcjd->pcid", tile_weights, carried, preferred_element_type=jnp.float32
    )
    return (products, present)


def add_rows(left, portion):
    return jnp.dot(left, portion, preferred_element_type=jnp.float32)


def shards(
    features,
    stripe_owner,
    dense_weight,
    sparse_weight,
    send_blocks,
    target_block,
    first_weight,
    second_weight,
):
    row_count, feature_width = features.shape
    block_rows = sparse_weight.shape[2]
    blocks_dev = row_count // block_rows
    stripe_count = stripe_owner.shape[1]
    narrow_index = lax.axis_index("narrow")
    wide_index = lax.axis_index("wide")
    owners = lax.dynamic_index_in_dim(stripe_owner, narrow_index, 0, keepdims=False)
    wide_rows = features.astype(jnp.float32)
    masked = jnp.stack(
        [
            jnp.where(owners[stripe_index] == wide_index, wide_rows, 0.0)
            for stripe_index in range(stripe_count)
        ]
    )
    stripes = (
        total_of(masked.astype(jnp.bfloat16), "wide")
        .astype(jnp.float32)
        .astype(jnp.bfloat16)
        .reshape(stripe_count * row_count, feature_width)
    )
    dense_sum = jnp.dot(
        dense_weight.astype(jnp.bfloat16), stripes, preferred_element_type=jnp.float32
    )
    tile_weights = sparse_weight[0].astype(jnp.bfloat16)
    listed = send_blocks[0]
    present = listed >= 0
    block_grid = features.reshape(blocks_dev, block_rows, feature_width)
    chosen = jnp.take(block_grid, jnp.maximum(listed, 0), axis=0)
    chosen = jnp.where(present[:, :, None, None], chosen, jnp.zeros((), jnp.bfloat16))
    products, arrived = tile_products(
        tile_weights,
        (
            lax.all_to_all(chosen, "narrow", split_axis=0, concat_axis=0, tiled=True),
            lax.all_to_all(
                present.astype(jnp.bfloat16), "narrow", split_axis=0, concat_axis=0, tiled=True
            ),
        ),
    )
    highest = lax.Precision.HIGHEST
    routed = (target_block[0][:, :, None] == jnp.arange(blocks_dev)[None, None, :]) & (
        arrived[:, :, None] > 0.5
    )
    routed = routed.astype(jnp.float32)
    sparse_sum = jnp.einsum("pcb,pcid->bid", routed, products, precision=highest).reshape(
        row_count, feature_width
    )
    row_weight = jnp.sum(sparse_weight[0], axis=2).astype(jnp.float32)
    sparse_degree = jnp.einsum("pcb,pi->bi", routed, row_weight, precision=highest).reshape(
        row_count
    )
    degree = 1.0 + jnp.sum(dense_weight, axis=1).astype(jnp.float32) + sparse_degree
    combined = (
        features.astype(jnp.float32) + (dense_sum + sparse_sum) / jnp.sqrt(degree)[:, None]
    ).astype(jnp.bfloat16)
    gated = add_rows(combined, lax.all_gather(first_weight, "wide", axis=0, tiled=True))
    hidden = jax.nn.relu(gated).astype(jnp.bfloat16)
    updated = add_rows(hidden, lax.all_gather(second_weight, "wide", axis=0, tiled=True))
    return updated.astype(jnp.bfloat16)


def solution(mesh):
    placed = (
        P(("wide", "narrow"), None),
        P(),
        P(("wide", "narrow"), None),
        P(("wide", "narrow"), None, None, None),
        P(("wide", "narrow"), None, None),
        P(("wide", "narrow"), None, None),
        P("wide", None),
        P("wide", None),
    )
    return jax.shard_map(
        shards, mesh=mesh, in_specs=placed, out_specs=P(("wide", "narrow"), None), check_vma=False
    )
```

profile of v0, /device:TPU:1, one launch (start us, length us, event | category | flops | bytes accessed | tf_op | source)
XLA Modules:
  0.0 398.9 jit_solution(15326536748898205373)
XLA Ops:
  6.5 0.0 copy-start
  6.5 0.7 convert_bitcast_fusion
  7.2 0.7 copy.38
  7.9 9.2 %all-to-all-start = ((bf16[16,1,2]{2,1,0:T(2,128)(2,1)}), bf16[16,1,2]{2,1,0:T(2,128)(2,1)S(1)}, u32[]{:S(2)}, u32[]{:S(2)}) async-start(bf16[16,1,2]{2,1,0:T(2,128)(2,1)} %copy.38), calls=%async_computation.1 | async-start | bytes 16384 | tf_op jit(solution)/shard_map/all_to_all | solution.py:75
  17.1 0.7 broadcast_maximum_fusion
  17.8 0.1 copy.40
  17.9 0.1 copy.41
  18.0 0.1 copy.42
  18.1 0.1 reshape.93
  18.2 3.8 gather_fusion
  22.0 6.4 %copy.43 = bf16[32,128,512]{1,2,0:T(8,128)(2,1)} copy(bf16[32,128,512]{2,1,0:T(8,128)(2,1)} %gather_fusion) | data formatting | bytes 8388608 | tf_op jit(solution)/shard_map/jit(_take)/gather | solution.py:69
  28.4 4.7 %select_select_fusion = bf16[16,2,128,512]{2,3,1,0:T(8,128)(2,1)} fusion(bf16[16,2,128,512]{2,3,1,0:T(8,128)(2,1)} %bitcast.57, pred[16,2]{1,0:T(8,128)(4,1)S(1)} %copy.41, pred[16,2]{1,0:T(8,128)(4,1)S(1)} %copy.40), kind=kLoop, calls=%fused_computation.2 | loop fusion | flops 4194304 | bytes 8388672 | tf_op jit(solution)/shard_map/jit(_where)/select_n | solution.py:70
  33.1 0.0 copy-start.1
  33.1 0.0 all-to-all-done
  33.1 7.1 %all-to-all-start.1 = ((bf16[16,2,128,512]{2,3,1,0:T(8,128)(2,1)}), bf16[16,2,128,512]{2,3,1,0:T(8,128)(2,1)}, u32[]{:S(2)}, u32[]{:S(2)}) async-start(bf16[16,2,128,512]{2,3,1,0:T(8,128)(2,1)} %select_select_fusion), calls=%async_computation.2 | async-start | bytes 8388608 | tf_op jit(solution)/shard_map/all_to_all | solution.py:74
  40.2 0.0 copy-start.2
  40.3 0.0 reduce-scatter.2.cloned.1.call-start
  40.3 0.0 copy-done.1
  40.3 0.2 copy.36
  40.5 0.0 copy-start.4
  40.5 0.0 copy-done
  40.6 0.1 constant_dynamic-slice_fusion
  40.6 0.7 fusion.20
  42.5 0.2 fusion.9
  42.7 0.0 copy-done.4
  42.7 0.0 copy-start.5
  42.7 0.1 pad_maximum_fusion
  42.8 1.3 copy.37
  44.1 0.0 reduce-scatter.2.cloned.1.call-update
  44.2 0.0 all-gather.4.cloned.1.call-start
  44.2 119.6 %reduce-scatter.2.cloned.1.call-done = bf16[32,512]{1,0:T(8,128)(2,1)} async-done(((bf16[1024,512]{1,0:T(8,128)(2,1)}), bf16[32,512]{1,0:T(8,128)(2,1)}) %reduce-scatter.2.cloned.1.call-update) | async-done | bytes 32784 | tf_op jit(solution)/shard_map/reduce_scatter | solution.py:15
  163.9 0.0 all-gather.4.cloned.1.call-update
  163.9 0.0 all-gather.6.cloned.1.call-start
  163.9 0.7 all-gather.6.cloned.1.call-update
  164.6 0.0 all-gather.8.cloned.1.call-start
  164.7 0.5 all-gather.8.cloned.1.call-update
  165.2 0.0 copy-done.2
  165.2 0.3 reduce_sum.29
  165.6 1.8 reduce_sum.27
  167.3 0.1 copy.39
  167.4 0.0 copy-done.5
  167.4 0.1 fusion.4
  167.6 0.0 all-to-all-done.1
  167.6 6.7 %convolution_bitcast_fusion = f32[16,2,128,512]{2,3,1,0:T(8,128)} fusion(bf16[16,2,128,512]{2,3,1,0:T(8,128)(2,1)} %all-to-all-done.1, s32[1,16,128,128]{3,2,1,0:T(8,128)S(1)} %copy-done.2), kind=kOutput, calls=%fused_computation.3 | convolution fusion | flops 537133056 | bytes 13631488 | tf_op jit(solution)/shard_map/pij,pcjd->pcid/dot_general | solution.py:22
  174.3 10.4 %copy.44 = f32[16,2,128,512]{3,0,1,2:T(8,128)} copy(f32[16,2,128,512]{2,3,1,0:T(8,128)} %convolution_bitcast_fusion) | data formatting | bytes 16777216 | tf_op jit(solution)/shard_map/pij,pcjd->pcid/transpose | solution.py:22
  184.6 5.6 %convolution_bitcast_fusion.1 = f32[4,128,512]{2,0,1:T(4,128)S(1)} fusion(f32[16,2,128,512]{3,0,1,2:T(8,128)} %copy.44, s32[16,2]{0,1:T(2,128)S(1)} %bitcast.61, pred[16,2]{0,1:T(4,128)(4,1)S(1)} %compare_bitcast_fusion.1), kind=kOutput, calls=%fused_computation.7 | convolution fusion | flops 100663552 | bytes 9437344 | tf_op jit(solution)/shard_map/pcb,pcid->bid/dot_general | solution.py:85
  190.3 0.0 copy-start.3
  190.3 0.3 copy.45
  190.6 1.3 copy.46
  191.9 43.5 %all-gather.4.cloned.1.call-done = bf16[1024,512]{1,0:T(8,128)(2,1)} async-done(((bf16[32,512]{1,0:T(8,128)(2,1)}), bf16[1024,512]{1,0:T(8,128)(2,1)}) %all-gather.4.cloned.1.call-update) | async-done | bytes 1048592 | tf_op jit(solution)/shard_map/all_gather | solution.py:16
  235.4 0.0 copy-done.3
  235.4 2.5 fusion.2
  237.9 73.1 %all-gather.6.cloned.1.call-done = bf16[512,2048]{1,0:T(8,128)(2,1)} async-done(((bf16[16,2048]{1,0:T(8,128)(2,1)}), bf16[512,2048]{1,0:T(8,128)(2,1)}) %all-gather.6.cloned.1.call-update) | async-done | bytes 2097168 | tf_op jit(solution)/shard_map/all_gather | solution.py:96
  311.0 76.0 %all-gather.8.cloned.1.call-done = bf16[2048,512]{1,0:T(8,128)(2,1)} async-done(((bf16[64,512]{1,0:T(8,128)(2,1)}), bf16[2048,512]{1,0:T(8,128)(2,1)}) %all-gather.8.cloned.1.call-update) | async-done | bytes 2097168 | tf_op jit(solution)/shard_map/all_gather | solution.py:98
  386.9 5.4 %convolution_convert_fusion = bf16[512,512]{1,0:T(8,128)(2,1)} fusion(bf16[2048,512]{1,0:T(8,128)(2,1)} %all-gather.8.cloned.1.call-done, bf16[512,512]{0,1:T(8,128)(2,1)S(1)} %fusion.2, bf16[512,2048]{1,0:T(8,128)(2,1)} %all-gather.6.cloned.1.call-done), kind=kOutput, calls=%fused_computation.11 | convolution fusion | flops 2149842944 | bytes 5242880 | tf_op jit(solution)/shard_map/dot_general | solution.py:29
  (3 shorter events, 0.0 us)
Async XLA Ops:
  6.5 34.0 %copy-start = (s32[16,2]{0,1:T(2,128)S(1)}, s32[16,2]{0,1:T(2,128)}, u32[]{:S(2)}) copy-start(s32[16,2]{0,1:T(2,128)} %param.9) | copy-start | bytes 388
  7.9 25.2 %all-to-all-start = ((bf16[16,1,2]{2,1,0:T(2,128)(2,1)}), bf16[16,1,2]{2,1,0:T(2,128)(2,1)S(1)}, u32[]{:S(2)}, u32[]{:S(2)}) async-start(bf16[16,1,2]{2,1,0:T(2,128)(2,1)} %copy.38), calls=%async_computation.1 | async-start | bytes 16384 | tf_op jit(solution)/shard_map/all_to_all | solution.py:75
  33.1 7.2 %copy-start.1 = (bf16[512,512]{1,0:T(8,128)(2,1)S(1)}, bf16[512,512]{1,0:T(8,128)(2,1)}, u32[]{:S(2)}) copy-start(bf16[512,512]{1,0:T(8,128)(2,1)} %param.8) | copy-start | bytes 1572868
  33.1 134.5 %all-to-all-start.1 = ((bf16[16,2,128,512]{2,3,1,0:T(8,128)(2,1)}), bf16[16,2,128,512]{2,3,1,0:T(8,128)(2,1)}, u32[]{:S(2)}, u32[]{:S(2)}) async-start(bf16[16,2,128,512]{2,3,1,0:T(8,128)(2,1)} %select_select_fusion), calls=%async_computation.2 | async-start | bytes 8388608 | tf_op jit(solution)/shard_map/all_to_all | solution.py:74
  40.2 125.0 %copy-start.2 = (s32[1,16,128,128]{3,2,1,0:T(8,128)S(1)}, s32[1,16,128,128]{3,2,1,0:T(8,128)}, u32[]{:S(2)}) copy-start(s32[1,16,128,128]{3,2,1,0:T(8,128)} %param.11) | copy-start | bytes 3145732
  40.3 123.6 %reduce-scatter.2.cloned.1.call-start = ((), (), s32[]{:S(2)}) async-start(), calls=%async_computation.3 | async-start | bytes 1081344 | tf_op jit(solution)/shard_map/reduce_scatter | solution.py:15
  40.5 2.2 copy-start.4
  42.7 124.7 %copy-start.5 = (s32[1,16,2]{1,2,0:T(2,128)S(1)}, s32[1,16,2]{1,2,0:T(2,128)}, u32[]{:S(2)}) copy-start(s32[1,16,2]{1,2,0:T(2,128)} %param.13) | copy-start | bytes 388
  44.2 191.2 %all-gather.4.cloned.1.call-start = ((), (), s32[]{:S(2)}) async-start(), calls=%async_computation.4 | async-start | bytes 1081344 | tf_op jit(solution)/shard_map/all_gather | solution.py:16
  163.9 147.1 %all-gather.6.cloned.1.call-start = ((), (), s32[]{:S(2)}) async-start(), calls=%async_computation.5 | async-start | bytes 2162688 | tf_op jit(solution)/shard_map/all_gather | solution.py:96
  164.6 222.3 %all-gather.8.cloned.1.call-start = ((), (), s32[]{:S(2)}) async-start(), calls=%async_computation.6 | async-start | bytes 2162688 | tf_op jit(solution)/shard_map/all_gather | solution.py:98
  190.3 45.1 %copy-start.3 = (s32[512,1024]{1,0:T(8,128)S(1)}, s32[512,1024]{1,0:T(8,128)}, u32[]{:S(2)}) copy-start(s32[512,1024]{1,0:T(8,128)} %param.10) | copy-start | bytes 6291460
Sparse Core Ops, SparseCore 0:
  45.4 118.3 reduce-scatter.1
  167.0 68.3 all-gather.3
  238.5 72.3 all-gather.5
  314.0 72.9 all-gather.7
where the time goes:
time: 400 us; the launch traced here: 399 us
  waiting for transfers between devices  313 us (78%)
  local copies, waits for them, and re-layouts  25.7 us (6%)
  matrix products  20.3 us (5%)
  starting transfers between devices  16.5 us (4%)
  between operations  14.5 us (4%)
  other arithmetic  8.46 us (2%)
    reduce_scatter x1, waiting for transfers between devices, total_of(): own = lax.psum_scatter(padded, axis, scatter_dimension=0, tiled=True)  120 us
    all_gather x1, waiting for transfers between devices, shards(): lax.all_gather(second_weight, 'wide', axis=0, tiled=True)  76 us
    all_gather x1, waiting for transfers between devices, shards(): lax.all_gather(first_weight, 'wide', axis=0, tiled=True)  73.1 us
    all_gather x1, waiting for transfers between devices, total_of(): whole = lax.all_gather(own, axis, axis=0, tiled=True)  43.5 us
    transpose x1, local copies, waits for them, and re-layouts, tile_products(): jnp.einsum('pij,pcjd->pcid', tile_weights, carried, preferred_element_typ...  10.4 us
    gather x2, local copies, waits for them, and re-layouts, shards(): chosen = jnp.take(block_grid, jnp.maximum(listed, 0), axis=0)  10.2 us
    all_to_all x1, starting transfers between devices, shards(): lax.all_to_all(present.astype(jnp.bfloat16), 'narrow', split_axis=0, conc...  9.17 us
  transfers between devices with their start and end apart: 6, of which 4 were waited for; matrix products, arithmetic and copies ran while one was open for 12% of the time, Pallas kernels for 0%

commit v1 on v0

--- a/solution.py
+++ b/solution.py
@@ -95,7 +95,13 @@
     ).astype(jnp.bfloat16)
     gated = add_rows(combined, lax.all_gather(first_weight, "wide", axis=0, tiled=True))
     hidden = jax.nn.relu(gated).astype(jnp.bfloat16)
-    updated = add_rows(hidden, lax.all_gather(second_weight, "wide", axis=0, tiled=True))
+
+    def check_sums_all(where_dim, xs, mesh_ax):
+        before = jnp.stack([xs for _ in range(lax.axis_size(mesh_ax))], axis=0)
+        arr_now = lax.all_to_all(before, mesh_ax, 0, 0)
+        return jnp.concatenate(arr_now, axis=where_dim)
+
+    updated = add_rows(hidden, check_sums_all(0, second_weight, "wide"))
     return updated.astype(jnp.bfloat16)
 
 

time: 400 us -> 454 us (1.14)
  waiting for transfers between devices: 313 us -> 349 us
  starting transfers between devices: 16.5 us -> 33.6 us
    all_to_all x1, waiting for transfers between devices: 0.01 us -> 96 us  [shards(): lax.all_to_all(chosen, 'narrow', split_axis=0, concat_axis=0, tiled=True)]
    all_gather x1 -> x0, waiting for transfers between devices: 76 us -> none  [shards(): lax.all_gather(second_weight, 'wide', axis=0, tiled=True)]
    all_to_all x0 -> x1, starting transfers between devices: none -> 17.1 us  [check_sums_all(): arr_now = lax.all_to_all(before, mesh_ax, 0, 0)]
    reduce_scatter x1, waiting for transfers between devices: 120 us -> 135 us  [total_of(): own = lax.psum_scatter(padded, axis, scatter_dimension=0, tiled=True)]
  transfers between devices with their start and end apart: 6 -> 6, of which waited for: 4 -> 4; matrix products, arithmetic and copies ran while one was open for 12% -> 11% of each run, Pallas kernels for 0% -> 0%
where the time goes in v1:
time: 454 us; the launch traced here: 453 us
  waiting for transfers between devices  349 us (77%)
  starting transfers between devices  33.6 us (7%)
  local copies, waits for them, and re-layouts  27.2 us (6%)
  matrix products  20.3 us (4%)
  between operations  14.5 us (3%)
  other arithmetic  8.48 us (2%)
    reduce_scatter x1, waiting for transfers between devices, total_of(): own = lax.psum_scatter(padded, axis, scatter_dimension=0, tiled=True)  135 us
    all_to_all x1, waiting for transfers between devices, shards(): lax.all_to_all(chosen, 'narrow', split_axis=0, concat_axis=0, tiled=True)  96 us
    all_gather x1, waiting for transfers between devices, shards(): lax.all_gather(first_weight, 'wide', axis=0, tiled=True)  73.1 us
    all_gather x1, waiting for transfers between devices, total_of(): whole = lax.all_gather(own, axis, axis=0, tiled=True)  44.1 us
    all_to_all x1, starting transfers between devices, check_sums_all(): arr_now = lax.all_to_all(before, mesh_ax, 0, 0)  17.1 us
    transpose x1, local copies, waits for them, and re-layouts, tile_products(): jnp.einsum('pij,pcjd->pcid', tile_weights, carried, preferred_element_typ...  10.4 us
    gather x2, local copies, waits for them, and re-layouts, shards(): chosen = jnp.take(block_grid, jnp.maximum(listed, 0), axis=0)  10.3 us
    all_to_all x1, starting transfers between devices, shards(): lax.all_to_all(present.astype(jnp.bfloat16), 'narrow', split_axis=0, conc...  9.17 us
  transfers between devices with their start and end apart: 6, of which 4 were waited for; matrix products, arithmetic and copies ran while one was open for 11% of the time, Pallas kernels for 0%

profile of v1, /device:TPU:1, one launch (start us, length us, event | category | flops | bytes accessed | tf_op | source)
XLA Modules:
  0.0 453.4 jit_solution(16186135347328983726)
XLA Ops:
  6.5 0.0 copy-start
  6.5 0.7 convert_bitcast_fusion
  7.2 0.7 copy.38
  7.9 9.2 %all-to-all-start = ((bf16[16,1,2]{2,1,0:T(2,128)(2,1)}), bf16[16,1,2]{2,1,0:T(2,128)(2,1)S(1)}, u32[]{:S(2)}, u32[]{:S(2)}) async-start(bf16[16,1,2]{2,1,0:T(2,128)(2,1)} %copy.38), calls=%async_computation.1 | async-start | bytes 16384 | tf_op jit(solution)/shard_map/all_to_all | solution.py:75
  17.1 0.7 broadcast_maximum_fusion
  17.8 0.1 copy.40
  17.9 0.1 copy.41
  18.0 0.1 copy.42
  18.1 0.1 reshape.99
  18.2 3.8 gather_fusion
  22.0 6.4 %copy.43 = bf16[32,128,512]{1,2,0:T(8,128)(2,1)} copy(bf16[32,128,512]{2,1,0:T(8,128)(2,1)} %gather_fusion) | data formatting | bytes 8388608 | tf_op jit(solution)/shard_map/jit(_take)/gather | solution.py:69
  28.4 4.7 %select_select_fusion = bf16[16,2,128,512]{2,3,1,0:T(8,128)(2,1)} fusion(bf16[16,2,128,512]{2,3,1,0:T(8,128)(2,1)} %bitcast.58, pred[16,2]{1,0:T(8,128)(4,1)S(1)} %copy.41, pred[16,2]{1,0:T(8,128)(4,1)S(1)} %copy.40), kind=kLoop, calls=%fused_computation.2 | loop fusion | flops 4194304 | bytes 8388672 | tf_op jit(solution)/shard_map/jit(_where)/select_n | solution.py:70
  33.1 0.0 copy-start.5
  33.1 0.0 all-to-all-done
  33.1 7.1 %all-to-all-start.1 = ((bf16[16,2,128,512]{2,3,1,0:T(8,128)(2,1)}), bf16[16,2,128,512]{2,3,1,0:T(8,128)(2,1)}, u32[]{:S(2)}, u32[]{:S(2)}) async-start(bf16[16,2,128,512]{2,3,1,0:T(8,128)(2,1)} %select_select_fusion), calls=%async_computation.2 | async-start | bytes 8388608 | tf_op jit(solution)/shard_map/all_to_all | solution.py:74
  40.3 0.0 copy-start.1
  40.3 0.0 copy-done
  40.3 0.1 constant_dynamic-slice_fusion
  40.4 96.0 %all-to-all-done.1 = bf16[16,2,128,512]{2,3,1,0:T(8,128)(2,1)} async-done(((bf16[16,2,128,512]{2,3,1,0:T(8,128)(2,1)}), bf16[16,2,128,512]{2,3,1,0:T(8,128)(2,1)}, u32[]{:S(2)}, u32[]{:S(2)}) %all-to-all-start.1) | async-done | bytes 4194336 | tf_op jit(solution)/shard_map/all_to_all | solution.py:74
  136.4 0.0 copy-done.5
  136.4 1.5 stack.14
  137.9 17.1 %all-to-all-start.2 = ((bf16[32,64,512]{2,1,0:T(8,128)(2,1)}), bf16[32,64,512]{2,1,0:T(8,128)(2,1)}, u32[]{:S(2)}, u32[]{:S(2)}) async-start(bf16[32,64,512]{2,1,0:T(8,128)(2,1)} %stack.14), calls=%async_computation.3 | async-start | bytes 4194304 | tf_op jit(solution)/shard_map/all_to_all | solution.py:101
  155.1 0.0 copy-start.2
  155.1 0.0 reduce-scatter.2.cloned.1.call-start
  155.2 0.5 fusion.20
  155.7 0.0 copy-done.1
  155.7 0.2 copy.36
  155.9 0.0 copy-start.4
  157.2 0.2 fusion.9
  157.3 0.0 copy-done.4
  157.4 0.0 copy-start.6
  157.4 0.1 pad_maximum_fusion
  157.5 1.4 copy.37
  158.8 0.0 reduce-scatter.2.cloned.1.call-update
  158.9 0.0 all-gather.3.cloned.1.call-start
  158.9 135.5 %reduce-scatter.2.cloned.1.call-done = bf16[32,512]{1,0:T(8,128)(2,1)} async-done(((bf16[1024,512]{1,0:T(8,128)(2,1)}), bf16[32,512]{1,0:T(8,128)(2,1)}) %reduce-scatter.2.cloned.1.call-update) | async-done | bytes 32784 | tf_op jit(solution)/shard_map/reduce_scatter | solution.py:15
  294.4 0.0 all-gather.3.cloned.1.call-update
  294.4 0.0 all-gather.5.cloned.1.call-start
  294.4 0.7 all-gather.5.cloned.1.call-update
  295.1 0.0 copy-done.2
  295.1 0.3 reduce_sum.29
  295.5 1.8 reduce_sum.27
  297.3 0.1 copy.39
  297.4 0.0 copy-done.6
  297.4 0.1 fusion.4
  297.5 6.7 %convolution_bitcast_fusion = f32[16,2,128,512]{2,3,1,0:T(8,128)} fusion(bf16[16,2,128,512]{2,3,1,0:T(8,128)(2,1)} %all-to-all-done.1, s32[1,16,128,128]{3,2,1,0:T(8,128)S(1)} %copy-done.2), kind=kOutput, calls=%fused_computation.3 | convolution fusion | flops 537133056 | bytes 13631488 | tf_op jit(solution)/shard_map/pij,pcjd->pcid/dot_general | solution.py:22
  304.2 10.4 %copy.44 = f32[16,2,128,512]{3,0,1,2:T(8,128)} copy(f32[16,2,128,512]{2,3,1,0:T(8,128)} %convolution_bitcast_fusion) | data formatting | bytes 16777216 | tf_op jit(solution)/shard_map/pij,pcjd->pcid/transpose | solution.py:22
  314.6 5.6 %convolution_bitcast_fusion.1 = f32[4,128,512]{2,0,1:T(4,128)S(1)} fusion(f32[16,2,128,512]{3,0,1,2:T(8,128)} %copy.44, s32[16,2]{0,1:T(2,128)S(1)} %bitcast.62, pred[16,2]{0,1:T(4,128)(4,1)S(1)} %compare_bitcast_fusion.1), kind=kOutput, calls=%fused_computation.7 | convolution fusion | flops 100663552 | bytes 9437344 | tf_op jit(solution)/shard_map/pcb,pcid->bid/dot_general | solution.py:85
  320.2 0.0 copy-start.3
  320.2 0.3 copy.45
  320.5 1.3 copy.46
  321.9 44.1 %all-gather.3.cloned.1.call-done = bf16[1024,512]{1,0:T(8,128)(2,1)} async-done(((bf16[32,512]{1,0:T(8,128)(2,1)}), bf16[1024,512]{1,0:T(8,128)(2,1)}) %all-gather.3.cloned.1.call-update) | async-done | bytes 1048592 | tf_op jit(solution)/shard_map/all_gather | solution.py:16
  365.9 0.0 copy-done.3
  365.9 2.5 fusion.2
  368.4 73.1 %all-gather.5.cloned.1.call-done = bf16[512,2048]{1,0:T(8,128)(2,1)} async-done(((bf16[16,2048]{1,0:T(8,128)(2,1)}), bf16[512,2048]{1,0:T(8,128)(2,1)}) %all-gather.5.cloned.1.call-update) | async-done | bytes 2097168 | tf_op jit(solution)/shard_map/all_gather | solution.py:96
  441.5 0.0 all-to-all-done.2
  441.5 5.4 %convolution_convert_fusion = bf16[512,512]{1,0:T(8,128)(2,1)} fusion(bf16[2048,512]{1,0:T(8,128)(2,1)} %bitcast.22, bf16[512,512]{0,1:T(8,128)(2,1)S(1)} %fusion.2, bf16[512,2048]{1,0:T(8,128)(2,1)} %all-gather.5.cloned.1.call-done), kind=kOutput, calls=%fused_computation.11 | convolution fusion | flops 2149842944 | bytes 5242880 | tf_op jit(solution)/shard_map/dot_general | solution.py:29
  (3 shorter events, 0.0 us)
Async XLA Ops:
  6.5 33.8 %copy-start = (s32[16,2]{0,1:T(2,128)S(1)}, s32[16,2]{0,1:T(2,128)}, u32[]{:S(2)}) copy-start(s32[16,2]{0,1:T(2,128)} %param.9) | copy-start | bytes 388
  7.9 25.2 %all-to-all-start = ((bf16[16,1,2]{2,1,0:T(2,128)(2,1)}), bf16[16,1,2]{2,1,0:T(2,128)(2,1)S(1)}, u32[]{:S(2)}, u32[]{:S(2)}) async-start(bf16[16,1,2]{2,1,0:T(2,128)(2,1)} %copy.38), calls=%async_computation.1 | async-start | bytes 16384 | tf_op jit(solution)/shard_map/all_to_all | solution.py:75
  33.1 103.3 %copy-start.5 = (bf16[64,512]{1,0:T(8,128)(2,1)S(1)}, bf16[64,512]{1,0:T(8,128)(2,1)}, u32[]{:S(2)}) copy-start(bf16[64,512]{1,0:T(8,128)(2,1)} %param.15) | copy-start | bytes 196612
  33.1 103.3 %all-to-all-start.1 = ((bf16[16,2,128,512]{2,3,1,0:T(8,128)(2,1)}), bf16[16,2,128,512]{2,3,1,0:T(8,128)(2,1)}, u32[]{:S(2)}, u32[]{:S(2)}) async-start(bf16[16,2,128,512]{2,3,1,0:T(8,128)(2,1)} %select_select_fusion), calls=%async_computation.2 | async-start | bytes 8388608 | tf_op jit(solution)/shard_map/all_to_all | solution.py:74
  40.3 115.4 %copy-start.1 = (bf16[512,512]{1,0:T(8,128)(2,1)S(1)}, bf16[512,512]{1,0:T(8,128)(2,1)}, u32[]{:S(2)}) copy-start(bf16[512,512]{1,0:T(8,128)(2,1)} %param.8) | copy-start | bytes 1572868
  137.9 303.6 %all-to-all-start.2 = ((bf16[32,64,512]{2,1,0:T(8,128)(2,1)}), bf16[32,64,512]{2,1,0:T(8,128)(2,1)}, u32[]{:S(2)}, u32[]{:S(2)}) async-start(bf16[32,64,512]{2,1,0:T(8,128)(2,1)} %stack.14), calls=%async_computation.3 | async-start | bytes 4194304 | tf_op jit(solution)/shard_map/all_to_all | solution.py:101
  155.1 140.0 %copy-start.2 = (s32[1,16,128,128]{3,2,1,0:T(8,128)S(1)}, s32[1,16,128,128]{3,2,1,0:T(8,128)}, u32[]{:S(2)}) copy-start(s32[1,16,128,128]{3,2,1,0:T(8,128)} %param.11) | copy-start | bytes 3145732
  155.1 139.3 %reduce-scatter.2.cloned.1.call-start = ((), (), s32[]{:S(2)}) async-start(), calls=%async_computation.4 | async-start | bytes 1081344 | tf_op jit(solution)/shard_map/reduce_scatter | solution.py:15
  155.9 1.4 copy-start.4
  157.4 140.0 %copy-start.6 = (s32[1,16,2]{1,2,0:T(2,128)S(1)}, s32[1,16,2]{1,2,0:T(2,128)}, u32[]{:S(2)}) copy-start(s32[1,16,2]{1,2,0:T(2,128)} %param.13) | copy-start | bytes 388
  158.9 207.1 %all-gather.3.cloned.1.call-start = ((), (), s32[]{:S(2)}) async-start(), calls=%async_computation.5 | async-start | bytes 1081344 | tf_op jit(solution)/shard_map/all_gather | solution.py:16
  294.4 147.1 %all-gather.5.cloned.1.call-start = ((), (), s32[]{:S(2)}) async-start(), calls=%async_computation.6 | async-start | bytes 2162688 | tf_op jit(solution)/shard_map/all_gather | solution.py:96
  320.2 45.7 %copy-start.3 = (s32[512,1024]{1,0:T(8,128)S(1)}, s32[512,1024]{1,0:T(8,128)}, u32[]{:S(2)}) copy-start(s32[512,1024]{1,0:T(8,128)} %param.10) | copy-start | bytes 6291460
Sparse Core Ops, SparseCore 0:
  160.3 134.0 reduce-scatter.1
  297.5 68.3 all-gather.2
  369.1 72.3 all-gather.4
